TPU v7x, 32 devices: a whole 2x2x4 slice. The times are simulated.
32 devices in a mesh: groups: 2 (over y), dom: 4 (over x, core), shard: 4 (over z).
Axes of the slice: x: 2, y: 2, z: 4, core: 2. Of those that a mesh axis runs over, the one named last changes fastest.
Arguments:
- rows: float32 [8, 8, 1152], P(('groups', 'dom'), 'shard'), parts along dimension 0, may hold values from -6 to 6
- targets: float32 [8, 8, 1152], P(('groups', 'dom'), 'shard'), parts along dimension 0, may hold values from -6 to 6
- w_gate: bfloat16 [4, 4608, 1152], P('dom', 'shard'), may hold values from -6 to 6
- w_up: bfloat16 [4, 4608, 1152], P('dom', 'shard'), may hold values from -6 to 6
- w_down: bfloat16 [4, 4608, 1152], P('dom', 'shard'), may hold values from -6 to 6
- member_at: int32 [2, 4], replicated, may hold values from 0 to 3, as said below
- lr_index: int32 [4], replicated, may hold values from 0 to 3
- rates: float32 [4], replicated, may hold values from 0.25 to 2
Outputs:
- pred: float32 [8, 8, 1152], P(('groups', 'dom'), 'shard'), parts along dimension 0
- grad_in: float32 [8, 8, 1152], P(('groups', 'dom'), 'shard'), parts along dimension 0
- new_gate: bfloat16 [8, 4608, 1152], P(('groups', 'dom'), 'shard'), parts along dimension 0
- new_up: bfloat16 [8, 4608, 1152], P(('groups', 'dom'), 'shard'), parts along dimension 0
- new_down: bfloat16 [8, 4608, 1152], P(('groups', 'dom'), 'shard'), parts along dimension 0
There are 2 independent parts, one for each index of `groups`. A program takes and returns all parts, laid end to end along the dimension named above; an argument that names none is the same for every part. Nothing has to cross between parts.
Inputs may be any that keep to these rules, and one draw needn't show every extreme that they name: Row 0 is a permutation of the members, and member_at[h, p] = member_at[0, (p - h) mod 4]: each member moves to the next partition at every step.
All inputs are finite; a program needn't handle non-finite values.
Results may differ from a plain program's by a relative error of at most 0.011.
Values may be sent and summed in bfloat16 or wider, within the bound.
No kernel may reach another device: no remote copies, remote signals or barrier semaphores. Data moves between devices by JAX's collectives and lax.ppermute only.
A program may use at most 64 MiB of HBM per device.

v0:
```python
import jax
import jax.numpy as jnp
from jax import lax
from jax.sharding import PartitionSpec as P

D = 1152
FF = 4608
HOPS = 2


def passed_along(value, axis, steps):
    count = lax.axis_size(axis)
    pairs = [(source, (source + steps) % count) for source in range(count)]
    return lax.ppermute(value, axis, pairs)


def lookup(table, wanted):
    positions = jnp.arange(table.shape[0], dtype=jnp.int32)
    return jnp.sum(jnp.where(positions == wanted, table, jnp.zeros_like(table)))


def member_rate(member_at, lr_index, rates, hop_index, position):
    member = lookup(member_at[hop_index], position)
    return lookup(rates, lookup(lr_index, member))


def local_pass(gathered, target_local, weights, step_rate, want_input):
    gate_w, up_w, down_w = weights
    scale_in = D ** (-0.5)
    scale_hidden = FF ** (-0.5)
    gate = (
        lax.dot_general(
            gathered, gate_w, (((1,), (1,)), ((), ())), preferred_element_type=jnp.float32
        )
        * scale_in
    )
    upward = (
        lax.dot_general(
            gathered, up_w, (((1,), (1,)), ((), ())), preferred_element_type=jnp.float32
        )
        * scale_in
    )
    sigma = jax.nn.sigmoid(gate)
    hidden = (gate * sigma * upward).astype(jnp.bfloat16)
    partial_out = jnp.dot(hidden, down_w, preferred_element_type=jnp.float32) * scale_hidden
    output = lax.psum_scatter(partial_out, "shard", scatter_dimension=0, tiled=True)
    resid_b = (output - target_local).astype(jnp.bfloat16)
    resid_all = lax.all_gather(resid_b, "shard", axis=0, tiled=True)
    d_hidden = (
        lax.dot_general(
            resid_all, down_w, (((1,), (1,)), ((), ())), preferred_element_type=jnp.float32
        )
        * scale_hidden
    )
    d_gate = (d_hidden * upward * sigma * (1.0 + gate * (1.0 - sigma))).astype(jnp.bfloat16)
    d_upward = (d_hidden * gate * sigma).astype(jnp.bfloat16)
    grad_down = (
        lax.dot_general(
            hidden, resid_all, (((0,), (0,)), ((), ())), preferred_element_type=jnp.float32
        )
        * scale_hidden
    )
    grad_gate = (
        lax.dot_general(
            d_gate, gathered, (((0,), (0,)), ((), ())), preferred_element_type=jnp.float32
        )
        * scale_in
    )
    grad_up = (
        lax.dot_general(
            d_upward, gathered, (((0,), (0,)), ((), ())), preferred_element_type=jnp.float32
        )
        * scale_in
    )
    d_partial = None
    if want_input:
        d_partial = (
            jnp.dot(d_gate, gate_w, preferred_element_type=jnp.float32)
            + jnp.dot(d_upward, up_w, preferred_element_type=jnp.float32)
        ) * scale_in
    new_gate = (gate_w.astype(jnp.float32) - step_rate * grad_gate).astype(jnp.bfloat16)
    new_up = (up_w.astype(jnp.float32) - step_rate * grad_up).astype(jnp.bfloat16)
    new_down = (down_w.astype(jnp.float32) - step_rate * grad_down).astype(jnp.bfloat16)
    return (output, d_partial, (new_gate, new_up, new_down))


def local(rows, targets, w_gate, w_up, w_down, member_at, lr_index, rates):
    position = lax.axis_index("dom")
    weights = (w_gate[0], w_up[0], w_down[0])
    inputs_local = rows[0]
    target_local = targets[0]
    gathered = lax.all_gather(inputs_local.astype(jnp.bfloat16), "shard", axis=0, tiled=True)
    for hop_index in range(HOPS):
        step_rate = member_rate(member_at, lr_index, rates, hop_index, position)
        output, d_partial, weights = local_pass(
            gathered, target_local, weights, step_rate, hop_index == HOPS - 1
        )
        weights = passed_along((weights[0], weights[1], weights[2]), "dom", 1)
    grad_local = lax.psum_scatter(d_partial, "shard", scatter_dimension=0, tiled=True)
    return (output[None], grad_local[None], weights[0][None], weights[1][None], weights[2][None])


def solution(mesh):
    return jax.shard_map(
        local,
        mesh=mesh,
        in_specs=(
            P(("groups", "dom"), "shard", None),
            P(("groups", "dom"), "shard", None),
            P("dom", "shard", None),
            P("dom", "shard", None),
            P("dom", "shard", None),
            P(),
            P(),
            P(),
        ),
        out_specs=(
            P(("groups", "dom"), "shard", None),
            P(("groups", "dom"), "shard", None),
            P(("groups", "dom"), "shard", None),
            P(("groups", "dom"), "shard", None),
            P(("groups", "dom"), "shard", None),
        ),
        check_vma=False,
    )
```

profile of v0, /device:TPU:0, one launch (start us, length us, event | category | flops | bytes accessed | tf_op | source)
XLA Modules:
  0.0 285.4 jit_solution(10826623407013125876)
XLA Ops:
  0.6 0.0 copy-start.1
  0.7 0.9 copy.17
  1.5 14.9 %all-gather = bf16[1,8,1152]{2,0,1:T(2,128)(2,1)S(1)} all-gather(bf16[1,2,1152]{2,0,1:T(2,128)(2,1)S(1)} %copy.17), channel_id=2, replica_groups=mesh['groups'=2,'dom'=4,'shard'=4] {'shard'}, dimensions={1}, use_global_device_ids=true | all-gather | bytes 23040 | tf_op jit(solution)/shard_map/all_gather | solution.py:92
  16.4 0.0 copy-start
  16.4 2.7 fusion.14
  19.1 0.0 copy-done.1
  19.1 0.0 copy-start.7
  19.1 0.0 copy-start.3
  19.1 0.8 multiply_convert_fusion.5
  19.9 0.0 copy-done
  19.9 0.0 copy-start.4
  19.9 0.0 copy-start.5
  19.9 0.0 copy-start.6
  20.0 0.5 fusion.20
  20.4 19.4 %all-reduce = f32[8,1152]{1,0:T(8,128)S(1)} all-reduce(f32[8,1152]{1,0:T(8,128)S(1)} %fusion.20), channel_id=3, replica_groups=mesh['groups'=2,'dom'=4,'shard'=4] {'shard'}, use_global_device_ids=true, to_apply=%region_0.1.clone | all-reduce | flops 9216 | bytes 73728
  39.8 0.0 copy-done.7
  39.8 0.6 dynamic-slice
  41.1 0.0 copy-done.3
  41.1 13.2 %all-gather.1 = bf16[4,2,1152]{2,1,0:T(2,128)(2,1)S(1)} all-gather(bf16[1,2,1152]{2,1,0:T(2,128)(2,1)S(1)} %fusion.42), channel_id=1, replica_groups=mesh['groups'=2,'dom'=4,'shard'=4] {'shard'}, dimensions={0}, use_global_device_ids=true | all-gather | bytes 23040 | tf_op jit(solution)/shard_map/all_gather | solution.py:48
  54.3 0.8 fusion.23
  55.1 0.0 copy-done.4
  55.1 0.7 fusion.44
  55.8 0.0 copy-done.5
  55.8 1.9 fusion.47
  57.7 0.0 copy-done.6
  57.7 1.9 fusion.48
  60.3 0.0 copy-start.2
  60.3 4.3 %fusion.3 = bf16[1152,1152]{1,0:T(8,128)(2,1)} fusion(bf16[1,1152,1152]{2,1,0:T(8,128)(2,1)} %param.10, f32[]{:T(128)S(6)} %mul.137, f32[8,1152]{1,0:T(8,128)S(1)} %fusion.14, f32[8,1152]{1,0:T(8,128)S(1)} %fusion.23, f32[8,1152]{1,0:T(8,128)S(1)} %get-tuple-element.16, bf16[1,8,1152]{2,1,0:T(8,128)(2,1)S(1)} %copy.15), kind=kOutput, calls=%fused_computation.9 | convolution fusion | flops 26634240 | bytes 5437444 | tf_op jit(solution)/shard_map/dot_general | solution.py:64
  64.6 0.0 collective-permute-start
  64.6 0.0 copy-done.2
  64.6 2.4 fusion.4
  67.1 1.6 collective-permute-start.1
  69.3 2.4 fusion.5
  71.7 0.0 collective-permute-start.2
  73.0 23.3 %collective-permute-done = bf16[1152,1152]{1,0:T(8,128)(2,1)} collective-permute-done((bf16[1152,1152]{1,0:T(8,128)(2,1)}, bf16[1152,1152]{1,0:T(8,128)(2,1)}, u32[]{:S(2)}, u32[]{:S(2)}) %collective-permute-start) | collective-permute-done | bytes 2654240 | tf_op jit(solution)/shard_map/ppermute | solution.py:14
  96.4 2.5 fusion.27
  98.9 25.9 %collective-permute-done.1 = bf16[1152,1152]{1,0:T(8,128)(2,1)} collective-permute-done((bf16[1152,1152]{1,0:T(8,128)(2,1)}, bf16[1152,1152]{1,0:T(8,128)(2,1)}, u32[]{:S(2)}, u32[]{:S(2)}) %collective-permute-start.1) | collective-permute-done | bytes 2654240 | tf_op jit(solution)/shard_map/ppermute | solution.py:14
  124.8 2.5 multiply_convert_fusion.2
  127.4 25.8 %collective-permute-done.2 = bf16[1152,1152]{1,0:T(8,128)(2,1)S(1)} collective-permute-done((bf16[1152,1152]{1,0:T(8,128)(2,1)}, bf16[1152,1152]{1,0:T(8,128)(2,1)S(1)}, u32[]{:S(2)}, u32[]{:S(2)}) %collective-permute-start.2) | collective-permute-done | bytes 2654240 | tf_op jit(solution)/shard_map/ppermute | solution.py:14
  153.1 0.5 convolution_multiply_fusion.7
  153.6 16.1 %all-reduce.1 = f32[8,1152]{1,0:T(8,128)S(1)} all-reduce(f32[8,1152]{1,0:T(8,128)S(1)} %convolution_multiply_fusion.7), channel_id=4, replica_groups=mesh['groups'=2,'dom'=4,'shard'=4] {'shard'}, use_global_device_ids=true, to_apply=%region_4.5.clone | all-reduce | flops 9216 | bytes 73728
  169.7 0.6 fusion.41
  170.3 13.2 %all-gather.2 = bf16[4,2,1152]{2,1,0:T(2,128)(2,1)S(1)} all-gather(bf16[1,2,1152]{2,1,0:T(2,128)(2,1)S(1)} %get-tuple-element.13), channel_id=1, replica_groups=mesh['groups'=2,'dom'=4,'shard'=4] {'shard'}, dimensions={0}, use_global_device_ids=true | all-gather | bytes 23040 | tf_op jit(solution)/shard_map/all_gather | solution.py:48
  183.5 0.8 multiply_convert_fusion.1
  184.3 4.2 %subtract_convert_fusion.2 = bf16[1152,1152]{1,0:T(8,128)(2,1)} fusion(bf16[1152,1152]{1,0:T(8,128)(2,1)} %collective-permute-done, f32[]{:T(128)S(6)} %mul.161, bf16[8,1152]{1,0:T(8,128)(2,1)S(1)} %get-tuple-element.11, bf16[1,8,1152]{2,1,0:T(8,128)(2,1)S(1)} %copy.15), kind=kOutput, calls=%fused_computation.14 | convolution fusion | flops 26542080 | bytes 5345284 | tf_op jit(solution)/shard_map/dot_general | solution.py:64
  188.5 0.0 collective-permute-start.3
  188.5 4.2 %subtract_convert_fusion.1 = bf16[1152,1152]{1,0:T(8,128)(2,1)} fusion(bf16[1152,1152]{1,0:T(8,128)(2,1)} %collective-permute-done.1, f32[]{:T(128)S(6)} %mul.161, bf16[8,1152]{1,0:T(8,128)(2,1)S(1)} %get-tuple-element.12, bf16[1,8,1152]{2,1,0:T(8,128)(2,1)S(1)} %copy.15), kind=kOutput, calls=%fused_computation.13 | convolution fusion | flops 26542080 | bytes 5345284 | tf_op jit(solution)/shard_map/dot_general | solution.py:70
  192.7 1.6 collective-permute-start.4
  194.3 2.4 subtract_convert_fusion
  196.7 0.0 collective-permute-start.5
  196.7 2.2 fusion.51
  198.9 2.2 fusion.26
  201.1 18.0 %all-reduce.2 = f32[8,1152]{1,0:T(8,128)S(1)} all-reduce(f32[8,1152]{1,0:T(8,128)S(1)} %fusion.26), channel_id=5, replica_groups=mesh['groups'=2,'dom'=4,'shard'=4] {'shard'}, use_global_device_ids=true, to_apply=%region_5.6.clone | all-reduce | flops 9216 | bytes 73728
  219.2 0.6 dynamic-slice_bitcast_fusion
  219.8 0.5 collective-permute-done.3
  220.3 28.4 %collective-permute-done.4 = bf16[1152,1152]{1,0:T(8,128)(2,1)} collective-permute-done((bf16[1152,1152]{1,0:T(8,128)(2,1)}, bf16[1152,1152]{1,0:T(8,128)(2,1)}, u32[]{:S(2)}, u32[]{:S(2)}) %collective-permute-start.4) | collective-permute-done | bytes 2654240 | tf_op jit(solution)/shard_map/ppermute | solution.py:14
  248.7 28.3 %collective-permute-done.5 = bf16[1152,1152]{1,0:T(8,128)(2,1)S(1)} collective-permute-done((bf16[1152,1152]{1,0:T(8,128)(2,1)}, bf16[1152,1152]{1,0:T(8,128)(2,1)S(1)}, u32[]{:S(2)}, u32[]{:S(2)}) %collective-permute-start.5) | collective-permute-done | bytes 2654240 | tf_op jit(solution)/shard_map/ppermute | solution.py:14
  277.0 3.5 %copy.21 = bf16[1,1152,1152]{2,1,0:T(8,128)(2,1)} copy(bf16[1,1152,1152]{2,1,0:T(8,128)(2,1)} %bitcast.12) | data formatting | bytes 5308416
  280.5 3.5 %copy.22 = bf16[1,1152,1152]{2,1,0:T(8,128)(2,1)} copy(bf16[1,1152,1152]{2,1,0:T(8,128)(2,1)} %bitcast.13) | data formatting | bytes 5308416
  283.9 1.5 copy.23
  (4 shorter events, 0.0 us)
Async XLA Ops:
  0.6 18.4 %copy-start.1 = (bf16[1,1152,1152]{2,1,0:T(8,128)(2,1)S(1)}, bf16[1,1152,1152]{2,1,0:T(8,128)(2,1)}, u32[]{:S(2)}) copy-start(bf16[1,1152,1152]{2,1,0:T(8,128)(2,1)} %param.11) | copy-start | bytes 7962628
  16.4 3.5 %copy-start = (bf16[1,1152,1152]{2,1,0:T(8,128)(2,1)S(1)}, bf16[1,1152,1152]{2,1,0:T(8,128)(2,1)}, u32[]{:S(2)}) copy-start(bf16[1,1152,1152]{2,1,0:T(8,128)(2,1)} %param.12) | copy-start | bytes 7962628
  19.1 20.8 %copy-start.7 = (u32[32]{0:T(128)S(1)}, u32[32]{0:T(128)}, u32[]{:S(2)}) copy-start(u32[32]{0:T(128)} %constant.26) | copy-start | bytes 388
  19.1 22.0 %copy-start.3 = (f32[1,2,1152]{2,1,0:T(2,128)S(1)}, f32[1,2,1152]{2,1,0:T(2,128)}, u32[]{:S(2)}) copy-start(f32[1,2,1152]{2,1,0:T(2,128)} %param.9) | copy-start | bytes 27652
  19.9 35.2 %copy-start.4 = (s32[2,4]{1,0:T(2,128)S(1)}, s32[2,4]{1,0:T(2,128)}, u32[]{:S(2)}) copy-start(s32[2,4]{1,0:T(2,128)} %param.13) | copy-start | bytes 100
  19.9 35.9 %copy-start.5 = (s32[4]{0:T(128)S(1)}, s32[4]{0:T(128)}, u32[]{:S(2)}) copy-start(s32[4]{0:T(128)} %param.14) | copy-start | bytes 52
  19.9 37.8 %copy-start.6 = (f32[4]{0:T(128)S(1)}, f32[4]{0:T(128)}, u32[]{:S(2)}) copy-start(f32[4]{0:T(128)} %param.15) | copy-start | bytes 52
  60.3 4.3 %copy-start.2 = (bf16[1,1152,1152]{2,1,0:T(8,128)(2,1)S(1)}, bf16[1,1152,1152]{2,1,0:T(8,128)(2,1)}, u32[]{:S(2)}) copy-start(bf16[1,1152,1152]{2,1,0:T(8,128)(2,1)} %param.11) | copy-start | bytes 7962628
  64.6 31.7 %collective-permute-start = (bf16[1152,1152]{1,0:T(8,128)(2,1)}, bf16[1152,1152]{1,0:T(8,128)(2,1)}, u32[]{:S(2)}, u32[]{:S(2)}) collective-permute-start(bf16[1152,1152]{1,0:T(8,128)(2,1)} %fusion.3), channel_id=1, source_target_pairs={{0,4},{4,8},{8,12},{12,0},{1,5},{5,9},{9,13},{13,1},{2,6},{6,10},{... | collective-permute-start | bytes 7962632 | tf_op jit(solution)/shard_map/ppermute | solution.py:14
  67.1 57.7 %collective-permute-start.1 = (bf16[1152,1152]{1,0:T(8,128)(2,1)}, bf16[1152,1152]{1,0:T(8,128)(2,1)}, u32[]{:S(2)}, u32[]{:S(2)}) collective-permute-start(bf16[1152,1152]{1,0:T(8,128)(2,1)} %fusion.4), channel_id=1, source_target_pairs={{0,4},{4,8},{8,12},{12,0},{1,5},{5,9},{9,13},{13,1},{2,6},{6,10},{... | collective-permute-start | bytes 7962632 | tf_op jit(solution)/shard_map/ppermute | solution.py:14
  71.7 81.4 %collective-permute-start.2 = (bf16[1152,1152]{1,0:T(8,128)(2,1)}, bf16[1152,1152]{1,0:T(8,128)(2,1)S(1)}, u32[]{:S(2)}, u32[]{:S(2)}) collective-permute-start(bf16[1152,1152]{1,0:T(8,128)(2,1)} %fusion.5), channel_id=1, source_target_pairs={{0,4},{4,8},{8,12},{12,0},{1,5},{5,9},{9,13},{13,1},{2,6},{6,10},{... | collective-permute-start | bytes 7962632 | tf_op jit(solution)/shard_map/ppermute | solution.py:14
  188.5 31.7 %collective-permute-start.3 = (bf16[1152,1152]{1,0:T(8,128)(2,1)}, bf16[1152,1152]{1,0:T(8,128)(2,1)}, u32[]{:S(2)}, u32[]{:S(2)}) collective-permute-start(bf16[1152,1152]{1,0:T(8,128)(2,1)} %subtract_convert_fusion.2), channel_id=1, source_target_pairs={{0,4},{4,8},{8,12},{12,0},{1,5},{5,9},{9,13},{13,1},{2,6},{6,10},{... | collective-permute-start | bytes 7962632 | tf_op jit(solution)/shard_map/ppermute | solution.py:14
  192.7 56.0 %collective-permute-start.4 = (bf16[1152,1152]{1,0:T(8,128)(2,1)}, bf16[1152,1152]{1,0:T(8,128)(2,1)}, u32[]{:S(2)}, u32[]{:S(2)}) collective-permute-start(bf16[1152,1152]{1,0:T(8,128)(2,1)} %subtract_convert_fusion.1), channel_id=1, source_target_pairs={{0,4},{4,8},{8,12},{12,0},{1,5},{5,9},{9,13},{13,1},{2,6},{6,10},{... | collective-permute-start | bytes 7962632 | tf_op jit(solution)/shard_map/ppermute | solution.py:14
  196.7 80.4 %collective-permute-start.5 = (bf16[1152,1152]{1,0:T(8,128)(2,1)}, bf16[1152,1152]{1,0:T(8,128)(2,1)S(1)}, u32[]{:S(2)}, u32[]{:S(2)}) collective-permute-start(bf16[1152,1152]{1,0:T(8,128)(2,1)} %subtract_convert_fusion), channel_id=1, source_target_pairs={{0,4},{4,8},{8,12},{12,0},{1,5},{5,9},{9,13},{13,1},{2,6},{6,10},{... | collective-permute-start | bytes 7962632 | tf_op jit(solution)/shard_map/ppermute | solution.py:14
where the time goes:
time: 286 us; the launch traced here: 285 us
  waiting for transfers between devices  132 us (46%)
  blocking collectives  94.8 us (33%)
  matrix products  35.5 us (12%)
  local copies, waits for them, and re-layouts  10.5 us (4%)
  other arithmetic  5.11 us (2%)
  between operations  4.03 us (1%)
  starting transfers between devices  3.22 us (1%)
    ppermute x6, waiting for transfers between devices, passed_along(): return lax.ppermute(value, axis, pairs)  132 us
    unnamed x3, blocking collectives  53.5 us
    all_gather x2, blocking collectives, local_pass(): resid_all = lax.all_gather(resid_b, 'shard', axis=0, tiled=True)  26.4 us
    all_gather x1, blocking collectives, local(): lax.all_gather(inputs_local.astype(jnp.bfloat16), 'shard', axis=0, tiled=...  14.9 us
    unnamed x24, local copies, waits for them, and re-layouts  9.93 us
    dot_general x2, matrix products, local_pass(): lax.dot_general(d_gate, gathered, (((0,), (0,)), ((), ())), preferred_ele...  8.51 us
    dot_general x2, matrix products, local_pass(): lax.dot_general(d_upward, gathered, (((0,), (0,)), ((), ())), preferred_e...  6.6 us
  transfers between devices with their start and end apart: 6, of which 6 were waited for; matrix products, arithmetic and copies ran while one was open for 8% of the time, Pallas kernels for 0%

commit v1 on v0

v1 whole, which is shorter than its diff:
```python
import functools

import jax
import jax.numpy as jnp
from jax import lax
from jax.experimental import pallas as pl
from jax.experimental.pallas import tpu as pltpu
from jax.sharding import PartitionSpec as P


BLOCK = 128
SMALL_RING = 8


def shifted(value, axis, steps):
    count = lax.axis_size(axis)
    pairs = [(source, (source + steps) % count) for source in range(count)]
    return lax.ppermute(value, axis, pairs)


def gathered_rows(value):
    count = lax.axis_size("shard")
    if count > SMALL_RING:
        return lax.all_gather(value, "shard", axis=0, tiled=True)
    parts = [value]
    for step in range(1, count):
        parts.append(shifted(value, "shard", step))
    return jnp.concatenate(parts, axis=0)


def summed_rows(partial):
    count = lax.axis_size("shard")
    if count > SMALL_RING:
        return lax.psum(partial, "shard")
    own = partial.shape[0] // count
    total = partial
    for step in range(1, count):
        got = shifted(partial, "shard", step)
        total = total + jnp.roll(got, step * own, axis=0)
    return total


def own_rows(full):
    count = lax.axis_size("shard")
    own = full.shape[0] // count
    if count > SMALL_RING:
        return lax.dynamic_slice_in_dim(full, lax.axis_index("shard") * own, own, 0)
    return full[:own]


def summed_own_rows(partial):
    count = lax.axis_size("shard")
    if count > SMALL_RING:
        return lax.psum_scatter(partial, "shard", scatter_dimension=0, tiled=True)
    own = partial.shape[0] // count
    total = partial[:own]
    for step in range(1, count):
        at = (count - step) * own
        total = total + shifted(partial[at : at + own], "shard", step)
    return total


def lookup(table, wanted):
    positions = jnp.arange(table.shape[0], dtype=jnp.int32)
    return jnp.sum(jnp.where(positions == wanted, table, jnp.zeros_like(table)))


def rate_of(member_at, lr_index, rates, step, partition):
    member = lookup(member_at[step], partition)
    return lookup(rates, lookup(lr_index, member))


def dot(a, b, dims):
    return lax.dot_general(a, b, (dims, ((), ())), preferred_element_type=jnp.float32)


def stepped(weight, left, right, rate):
    grad = dot(left, right, ((0,), (0,)))
    return (weight.astype(jnp.float32) - rate * grad).astype(jnp.bfloat16)


def block_kernel(entries, hops, left_at, right_at, at_ref, rate_ref, *refs):
    count = len(entries)
    packs, blocks = refs[:hops], refs[hops : hops + count]
    wide = blocks[0].shape[1]
    out_ref, done, sems = refs[-3:]
    copies = []
    for index, (first, second) in enumerate(entries):
        at = jnp.where(at_ref[0] == 0, first, second)
        start = pl.multiple_of(at * BLOCK, BLOCK)
        value = blocks[index][...]
        for hop in range(hops):
            left = packs[hop][:, pl.ds(pl.multiple_of(left_at + start, BLOCK), BLOCK)]
            right = packs[hop][:, right_at : right_at + wide]
            value = stepped(value, left, right, rate_ref[hop])
        done[index] = value
        copy = pltpu.make_async_copy(
            done.at[index], out_ref.at[pl.ds(start, BLOCK), :], sems.at[index]
        )
        copy.start()
        copies.append(copy)
    for copy in copies:
        copy.wait()


def updated_blocks(at, rate, packs, sides, blocks, entries, shape, before=None):
    hops = len(packs)
    vmem = pl.BlockSpec(memory_space=pltpu.VMEM)
    smem = pl.BlockSpec(memory_space=pltpu.SMEM)
    anywhere = pl.BlockSpec(memory_space=pl.ANY)
    count = len(blocks)
    carried = [] if before is None else [before]
    return pl.pallas_call(
        functools.partial(block_kernel, entries, hops, *sides),
        out_shape=jax.ShapeDtypeStruct(shape, jnp.bfloat16),
        in_specs=[smem, smem] + [vmem] * (hops + count) + [anywhere] * len(carried),
        out_specs=anywhere,
        scratch_shapes=[
            pltpu.VMEM((count, BLOCK, shape[1]), jnp.bfloat16),
            pltpu.SemaphoreType.DMA((count,)),
        ],
        input_output_aliases={} if before is None else {2 + hops + count: 0},
        cost_estimate=pl.CostEstimate(
            flops=4 * hops * count * BLOCK * shape[1] * packs[0].shape[0],
            bytes_accessed=4 * count * BLOCK * shape[1],
            transcendentals=0,
        ),
        compiler_params=pltpu.CompilerParams(vmem_limit_bytes=24 * 2**20),
        name="apply_steps",
    )(at, rate, *packs, *blocks, *carried)


def forward(inputs, weights):
    gate_w, up_w, down_w = weights
    scale_in = gate_w.shape[1] ** (-0.5)
    gate = dot(inputs, gate_w, ((1,), (1,))) * scale_in
    upward = dot(inputs, up_w, ((1,), (1,))) * scale_in
    sigma = jax.nn.sigmoid(gate)
    hidden = (gate * sigma * upward).astype(jnp.bfloat16)
    partial_out = dot(hidden, down_w, ((1,), (0,)))
    return gate, upward, sigma, hidden, partial_out


def backward(resid, down_w, gate, upward, sigma, scale_hidden):
    d_hidden = dot(resid, down_w, ((1,), (1,))) * scale_hidden
    d_gate = (d_hidden * upward * sigma * (1.0 + gate * (1.0 - sigma))).astype(jnp.bfloat16)
    d_upward = (d_hidden * gate * sigma).astype(jnp.bfloat16)
    return d_gate, d_upward


def local(rows, targets, w_gate, w_up, w_down, member_at, lr_index, rates):
    return local_body(
        rows[0], targets[0], (w_gate[0], w_up[0], w_down[0]), member_at, lr_index, rates
    )


def local_body(rows, targets, weights, member_at, lr_index, rates):
    hops = member_at.shape[0]
    parts = lax.axis_size("dom")
    position = lax.axis_index("dom")
    group = lax.axis_index("groups")
    tall, wide = weights[0].shape
    hidden_units = tall * lax.axis_size("shard")
    scale_in = wide ** (-0.5)
    scale_hidden = hidden_units ** (-0.5)
    start = weights
    relayed = lax.axis_size("groups") == 2 and tall % BLOCK == 0 and tall >= BLOCK

    local_data = jnp.concatenate([rows, targets], axis=0)
    own = rows.shape[0]
    visits = [local_data]
    for hop in range(1, hops):
        visits.append(shifted(local_data, "dom", -hop))

    nblocks = tall // BLOCK if relayed else 0
    pairs, arrived = [], []
    if relayed:
        leftovers = [(m, nblocks - 1) for m in range(3)] if nblocks % 2 else []
        pairs = [((m, 2 * j), (m, 2 * j + 1)) for m in range(3) for j in range(nblocks // 2)]
        if leftovers:
            pairs.insert(2 * (nblocks // 2), (leftovers[0], leftovers[1]))
        direct = leftovers[2:]

        def block(which):
            m, b = which
            return lax.slice_in_dim(start[m], b * BLOCK, (b + 1) * BLOCK, axis=0)

        for first, second in pairs:
            if first[0] == second[0]:
                mine = lax.dynamic_slice_in_dim(
                    start[first[0]], (first[1] + group) * BLOCK, BLOCK, 0
                )
            else:
                mine = jnp.where(group == 0, block(first), block(second))
            got = shifted(mine, "dom", hops)
            other = shifted(got, "groups", 1)
            arrived.append((got, other))
        directly = []
        for which in direct:
            directly.append(shifted(block(which), "dom", hops))

    packs = []
    for hop in range(hops):
        last = hop == hops - 1
        data = gathered_rows(visits[hop])
        count = data.shape[0] // (2 * own)
        data = data.reshape(count, 2, own, wide)
        inputs = data[:, 0].reshape(count * own, wide).astype(jnp.bfloat16)
        wanted = data[:, 1].reshape(count * own, wide)
        gate, upward, sigma, hidden, partial_out = forward(inputs, weights)
        output = summed_rows(partial_out * scale_hidden)
        resid = (output - wanted).astype(jnp.bfloat16)
        d_gate, d_upward = backward(resid, weights[2], gate, upward, sigma, scale_hidden)
        packs.append(jnp.concatenate([d_gate, d_upward, hidden, inputs, resid], axis=1))
        if not last:
            rate = rate_of(member_at, lr_index, rates, hop, (position + hop) % parts)
            weights = (
                stepped(weights[0], d_gate, inputs, rate * scale_in),
                stepped(weights[1], d_upward, inputs, rate * scale_in),
                stepped(weights[2], hidden, resid, rate * scale_hidden),
            )
        else:
            d_partial = (
                dot(d_gate, weights[0], ((1,), (0,))) + dot(d_upward, weights[1], ((1,), (0,)))
            ) * scale_in
            grad_own = summed_own_rows(d_partial)
            results = jnp.concatenate([own_rows(output), grad_own], axis=0)
            results = shifted(results, "dom", hops - 1)
    came = []
    for hop in range(hops):
        came.append(shifted(packs[hop], "dom", hops))

    home = (position - hops) % parts
    rate = jnp.stack(
        [rate_of(member_at, lr_index, rates, hop, (home + hop) % parts) for hop in range(hops)]
    )
    scales = (scale_in, scale_in, scale_hidden)
    sides = tuple((m * tall, 3 * tall + (m // 2) * wide) for m in range(3))
    news = []
    if relayed:
        at = group.reshape(1).astype(jnp.int32)
        for m in range(3):
            blocks, entries = [], []
            for (first, second), (got, other) in zip(pairs, arrived):
                if first[0] == second[0] == m:
                    blocks += [got, other]
                    entries += [(first[1], second[1]), (second[1], first[1])]
                elif first[0] == m:
                    blocks.append(jnp.where(group == 0, got, other))
                    entries.append((first[1], first[1]))
                elif second[0] == m:
                    blocks.append(jnp.where(group == 0, other, got))
                    entries.append((second[1], second[1]))
            for which, got in zip(direct, directly):
                if which[0] == m:
                    blocks.append(got)
                    entries.append((which[1], which[1]))
            cut = len(blocks) - 3 if m == 2 and len(blocks) > 3 else len(blocks)
            new = updated_blocks(
                at, rate * scales[m], came, sides[m], blocks[:cut], entries[:cut], (tall, wide)
            )
            if cut < len(blocks):
                new = updated_blocks(
                    at, rate * scales[m], came, sides[m], blocks[cut:], entries[cut:], (tall, wide), new
                )
            news.append(new)
    else:
        for m in range(3):
            new = shifted(start[m], "dom", hops)
            for hop in range(hops):
                left_at, right_at = sides[m]
                left = came[hop][:, left_at : left_at + tall]
                right = came[hop][:, right_at : right_at + wide]
                new = stepped(new, left, right, rate[hop] * scales[m])
            news.append(new)
    return (results[None, :own], results[None, own:], news[0][None], news[1][None], news[2][None])


def solution(mesh):
    return jax.shard_map(
        local,
        mesh=mesh,
        in_specs=(
            P(("groups", "dom"), "shard", None),
            P(("groups", "dom"), "shard", None),
            P("dom", "shard", None),
            P("dom", "shard", None),
            P("dom", "shard", None),
            P(),
            P(),
            P(),
        ),
        out_specs=(P(("groups", "dom"), "shard", None),) * 5,
        check_vma=False,
    )
```

time: 286 us -> 207 us (0.72)
  blocking collectives: 94.8 us -> 0 us
  starting transfers between devices: 3.22 us -> 52.2 us
  waiting for transfers between devices: 132 us -> 107 us
  matrix products: 35.5 us -> 14.6 us
  Pallas kernels: 0 us -> 10.2 us
  other arithmetic: 5.11 us -> 14.3 us
  local copies, waits for them, and re-layouts: 10.5 us -> 5.17 us
    unnamed x3 -> x0, blocking collectives: 53.5 us -> none
    ppermute x6 -> x46, starting transfers between devices: 3.22 us -> 52.2 us  [shifted(): return lax.ppermute(value, axis, pairs)]
    all_gather x3 -> x0, blocking collectives: 41.3 us -> none  [the longest x2 26.4 us: local_pass(): resid_all = lax.all_gather(resid_b, 'shard', axis=0, tiled=True)]
    ppermute x6 -> x46, waiting for transfers between devices: 132 us -> 107 us  [shifted(): return lax.ppermute(value, axis, pairs)]
    dot_general x16 -> x13, matrix products: 35.5 us -> 14.6 us  [dot(): lax.dot_general(a, b, (dims, ((), ())), preferred_element_type=jnp.float32)]
    pallas_call x0 -> x4, Pallas kernels: none -> 10.2 us  [updated_blocks(): pl.pallas_call(functools.partial(block_kernel, entries, hops, *sides), ou...]
    unnamed x24 -> x37, local copies, waits for them, and re-layouts: 9.93 us -> 0.92 us
    dynamic_slice x0 -> x1, other arithmetic: none -> 3.33 us  [local_body(): lax.dynamic_slice_in_dim(start[first[0]], (first[1] + group) * BLOCK, BLO...]
  transfers between devices with their start and end apart: 6 -> 46, of which waited for: 6 -> 28; matrix products, arithmetic and copies ran while one was open for 8% -> 16% of each run, Pallas kernels for 0% -> 4%
where the time goes in v1:
time: 207 us; the launch traced here: 206 us
  waiting for transfers between devices  107 us (52%)
  starting transfers between devices  52.2 us (25%)
  matrix products  14.6 us (7%)
  other arithmetic  14.3 us (7%)
  Pallas kernels  10.2 us (5%)
  local copies, waits for them, and re-layouts  5.17 us (2%)
  between operations  2.47 us (1%)
    ppermute x46, waiting for transfers between devices, shifted(): return lax.ppermute(value, axis, pairs)  107 us
    ppermute x46, starting transfers between devices, shifted(): return lax.ppermute(value, axis, pairs)  52.2 us
    dot_general x13, matrix products, dot(): lax.dot_general(a, b, (dims, ((), ())), preferred_element_type=jnp.float32)  14.6 us
    pallas_call x4, Pallas kernels, updated_blocks(): pl.pallas_call(functools.partial(block_kernel, entries, hops, *sides), ou...  10.2 us
    reduce_sum x3, other arithmetic, lookup(): return jnp.sum(jnp.where(positions == wanted, table, jnp.zeros_like(table)))  5.81 us
  transfers between devices with their start and end apart: 46, of which 28 were waited for; matrix products, arithmetic and copies ran while one was open for 16% of the time, Pallas kernels for 4%

profile of v1, /device:TPU:0, one launch (start us, length us, event | category | flops | bytes accessed | tf_op | source)
XLA Modules:
  0.0 205.7 jit_solution(6348664320434339392)
XLA Ops:
  1.4 2.5 %collective-permute-start = (f32[4,1152]{1,0:T(4,128)S(1)}, f32[4,1152]{1,0:T(4,128)S(1)}, u32[]{:S(2)}, u32[]{:S(2)}) collective-permute-start(f32[4,1152]{1,0:T(4,128)S(1)} %pad_maximum_fusion.1), channel_id=1, source_target_pairs={{0,12},{4,0},{8,4},{12,8},{1,13},{5,1},{9,5},{13,9},{2,14},{6,2},{... | collective-permute-start | bytes 55304 | tf_op jit(solution)/shard_map/ppermute | solution.py:18
  3.8 1.6 collective-permute-start.4
  5.4 2.6 %collective-permute-start.5 = (f32[4,1152]{1,0:T(4,128)S(1)}, f32[4,1152]{1,0:T(4,128)S(1)}, u32[]{:S(2)}, u32[]{:S(2)}) collective-permute-start(f32[4,1152]{1,0:T(4,128)S(1)} %pad_maximum_fusion.1), channel_id=1, source_target_pairs={{0,2},{1,3},{2,0},{3,1},{4,6},{5,7},{6,4},{7,5},{8,10},{9,11},{10,... | collective-permute-start | bytes 55304 | tf_op jit(solution)/shard_map/ppermute | solution.py:18
  8.0 1.3 collective-permute-start.6
  9.4 3.3 %dynamic-slice_bitcast_fusion.4 = (bf16[128,1152]{1,0:T(8,128)(2,1)}, bf16[128,1152]{1,0:T(8,128)(2,1)}, bf16[128,1152]{1,0:T(8,128)(2,1)}, bf16[128,1152]{1,0:T...) fusion(bf16[1,1152,1152]{2,1,0:T(8,128)(2,1)} %param.11, ...), kind=kLoop, calls=%fused_computation.32 | loop fusion | flops 147456 | bytes 5603345 | tf_op jit(solution)/shard_map/dynamic_slice | solution.py:190
  14.0 2.7 %fusion.40 = (s32[]{:T(128)}, s32[]{:T(128)}, s32[]{:T(128)}) fusion(s32[4]{0:T(128)S(1)} %copy-done.13, s32[]{:T(128)} %get-tuple-element.5, s32[]{:T(128)} %get-tuple-element.7, s32[]{:T(128)} %get-tuple-element.6), kind=kLoop, calls=%fused_computation.95 | loop fusion | flops 33 | bytes 40 | tf_op jit(solution)/shard_map/reduce_sum | solution.py:65
  16.7 2.4 %fusion.41 = (f32[]{:T(128)}, f32[]{:T(128)}, f32[]{:T(128)}) fusion(f32[4]{0:T(128)S(1)} %copy-done.14, s32[]{:T(128)} %get-tuple-element.11, s32[]{:T(128)} %get-tuple-element.12, s32[]{:T(128)} %get-tuple-element.13), kind=kLoop, calls=%fused_computation.96 | loop fusion | flops 33 | bytes 40 | tf_op jit(solution)/shard_map/reduce_sum | solution.py:65
  20.4 1.5 collective-permute-start.21
  22.1 2.7 %fusion.14 = f32[8,1152]{1,0:T(8,128)S(1)} fusion(bf16[8,1152]{1,0:T(8,128)(2,1)S(1)} %convert_element_type.57, bf16[1,1152,1152]{2,1,0:T(8,128)(2,1)} %param.10), kind=kOutput, calls=%fused_computation.17 | convolution fusion | flops 21242880 | bytes 2709504 | tf_op jit(solution)/shard_map/dot_general | solution.py:74
  24.8 3.2 %multiply_convert_fusion.5 = (bf16[8,1152]{1,0:T(8,128)(2,1)S(1)}, f32[8,1152]{1,0:T(8,128)}) fusion(f32[8,1152]{1,0:T(8,128)S(1)} %fusion.14, bf16[8,1152]{1,0:T(8,128)(2,1)S(1)} %convert_element_type.57, bf16[1,1152,1152]{2,1,0:T(8,128)(2,1)} %param.11), kind=kOutput, calls=%fused_computation.63 | convolution fusion | flops 21298176 | bytes 2764800 | tf_op jit(solution)/shard_map/dot_general | solution.py:74
  28.5 1.7 collective-permute-start.2
  30.9 0.9 collective-permute-done.3
  33.1 2.0 collective-permute-start.8
  35.8 1.3 collective-permute-start.9
  38.0 1.9 collective-permute-done.9
  42.2 0.9 fusion.48
  43.9 1.6 constant_dynamic-update-slice_fusion.4
  45.5 0.9 fusion.3
  47.2 0.9 fusion.4
  48.2 0.9 fusion.5
  49.9 0.8 multiply_convert_fusion.2
  51.2 3.1 %collective-permute-start.12 = (f32[8,1152]{1,0:T(8,128)S(1)}, f32[8,1152]{1,0:T(8,128)S(1)}, u32[]{:S(2)}, u32[]{:S(2)}) collective-permute-start(f32[8,1152]{1,0:T(8,128)S(1)} %convolution_multiply_fusion.4), channel_id=1, source_target_pairs={{0,3},{1,0},{2,1},{3,2},{4,7},{5,4},{6,5},{7,6},{8,11},{9,8},{10,9... | collective-permute-start | bytes 110600 | tf_op jit(solution)/shard_map/ppermute | solution.py:18
  55.0 4.2 %collective-permute-done.11 = f32[8,1152]{1,0:T(8,128)S(1)} collective-permute-done((f32[8,1152]{1,0:T(8,128)S(1)}, f32[8,1152]{1,0:T(8,128)S(1)}, u32[]{:S(2)}, u32[]{:S(2)}) %collective-permute-start.11) | collective-permute-done | bytes 36896 | tf_op jit(solution)/shard_map/ppermute | solution.py:18
  59.2 0.8 collective-permute-done.10
  63.4 1.9 collective-permute-start.13
  67.8 1.0 collective-permute-done.13
  69.1 3.2 %collective-permute-done.16 = f32[4,1152]{1,0:T(4,128)S(1)} collective-permute-done((f32[4,1152]{1,0:T(4,128)S(1)}, f32[4,1152]{1,0:T(4,128)S(1)}, u32[]{:S(2)}, u32[]{:S(2)}) %collective-permute-start.16) | collective-permute-done | bytes 18464 | tf_op jit(solution)/shard_map/ppermute | solution.py:18
  73.0 1.3 collective-permute-start.25
  75.1 1.3 collective-permute-start.29
  77.2 5.0 %collective-permute-done.23.refs_6_ = bf16[128,1152]{1,0:T(8,128)(2,1)S(1)} collective-permute-done((bf16[128,1152]{1,0:T(8,128)(2,1)S(1)}, bf16[128,1152]{1,0:T(8,128)(2,1)S(1)}, u32[]{:S(2)}, u32[]{:S(2)}) %collective-permute-start.23) | collective-permute-done | bytes 294944 | tf_op jit(solution)/shard_map/ppermute | solution.py:18
  82.9 5.6 %collective-permute-done.25.refs_8_ = bf16[128,1152]{1,0:T(8,128)(2,1)S(1)} collective-permute-done((bf16[128,1152]{1,0:T(8,128)(2,1)S(1)}, bf16[128,1152]{1,0:T(8,128)(2,1)S(1)}, u32[]{:S(2)}, u32[]{:S(2)}) %collective-permute-start.25) | collective-permute-done | bytes 294944 | tf_op jit(solution)/shard_map/ppermute | solution.py:18
  89.2 5.6 %collective-permute-done.27 = bf16[128,1152]{1,0:T(8,128)(2,1)S(1)} collective-permute-done((bf16[128,1152]{1,0:T(8,128)(2,1)S(1)}, bf16[128,1152]{1,0:T(8,128)(2,1)S(1)}, u32[]{:S(2)}, u32[]{:S(2)}) %collective-permute-start.27) | collective-permute-done | bytes 294944 | tf_op jit(solution)/shard_map/ppermute | solution.py:18
  95.5 5.6 %collective-permute-done.29.refs_2_ = bf16[128,1152]{1,0:T(8,128)(2,1)S(1)} collective-permute-done((bf16[128,1152]{1,0:T(8,128)(2,1)S(1)}, bf16[128,1152]{1,0:T(8,128)(2,1)S(1)}, u32[]{:S(2)}, u32[]{:S(2)}) %collective-permute-start.29) | collective-permute-done | bytes 294944 | tf_op jit(solution)/shard_map/ppermute | solution.py:18
  101.9 5.6 %collective-permute-done.31.refs_4_ = bf16[128,1152]{1,0:T(8,128)(2,1)S(1)} collective-permute-done((bf16[128,1152]{1,0:T(8,128)(2,1)S(1)}, bf16[128,1152]{1,0:T(8,128)(2,1)S(1)}, u32[]{:S(2)}, u32[]{:S(2)}) %collective-permute-start.31) | collective-permute-done | bytes 294944 | tf_op jit(solution)/shard_map/ppermute | solution.py:18
  108.2 5.6 %collective-permute-done.33.refs_6_ = bf16[128,1152]{1,0:T(8,128)(2,1)S(1)} collective-permute-done((bf16[128,1152]{1,0:T(8,128)(2,1)S(1)}, bf16[128,1152]{1,0:T(8,128)(2,1)S(1)}, u32[]{:S(2)}, u32[]{:S(2)}) %collective-permute-start.33) | collective-permute-done | bytes 294944 | tf_op jit(solution)/shard_map/ppermute | solution.py:18
  114.5 5.6 %collective-permute-done.37.refs_2_ = bf16[128,1152]{1,0:T(8,128)(2,1)S(1)} collective-permute-done((bf16[128,1152]{1,0:T(8,128)(2,1)S(1)}, bf16[128,1152]{1,0:T(8,128)(2,1)S(1)}, u32[]{:S(2)}, u32[]{:S(2)}) %collective-permute-start.37) | collective-permute-done | bytes 294944 | tf_op jit(solution)/shard_map/ppermute | solution.py:18
  120.1 1.5 collective-permute-start.38
  121.6 4.8 %collective-permute-done.40.refs_2_ = bf16[128,1152]{1,0:T(8,128)(2,1)S(1)} collective-permute-done((bf16[128,1152]{1,0:T(8,128)(2,1)S(1)}, bf16[128,1152]{1,0:T(8,128)(2,1)S(1)}, u32[]{:S(2)}, u32[]{:S(2)}) %collective-permute-start.40) | collective-permute-done | bytes 294944 | tf_op jit(solution)/shard_map/ppermute | solution.py:18
  126.4 1.5 collective-permute-start.41
  127.9 4.8 %collective-permute-done.42.refs_4_ = bf16[128,1152]{1,0:T(8,128)(2,1)S(1)} collective-permute-done((bf16[128,1152]{1,0:T(8,128)(2,1)S(1)}, bf16[128,1152]{1,0:T(8,128)(2,1)S(1)}, u32[]{:S(2)}, u32[]{:S(2)}) %collective-permute-start.42) | collective-permute-done | bytes 294944 | tf_op jit(solution)/shard_map/ppermute | solution.py:18
  132.7 1.5 collective-permute-start.43
  134.3 4.8 %collective-permute-done.44.refs_6_ = bf16[128,1152]{1,0:T(8,128)(2,1)S(1)} collective-permute-done((bf16[128,1152]{1,0:T(8,128)(2,1)S(1)}, bf16[128,1152]{1,0:T(8,128)(2,1)S(1)}, u32[]{:S(2)}, u32[]{:S(2)}) %collective-permute-start.44) | collective-permute-done | bytes 294944 | tf_op jit(solution)/shard_map/ppermute | solution.py:18
  139.1 1.5 collective-permute-start.45
  140.6 1.3 broadcast_multiply_fusion.1.rate_ref
  141.9 1.3 broadcast_multiply_fusion.rate_ref
  143.3 1.0 collective-permute-start.35
  144.3 1.5 collective-permute-start.20
  146.3 1.5 collective-permute-start.24
  148.9 2.4 %apply_steps.6.refs_5_ = bf16[1152,1152]{1,0:T(8,128)(2,1)} custom-call(s32[1]{0:T(128)} %bitcast.8.at_ref, f32[2]{0:T(128)S(1)} %broadcast_multiply_fusion.rate_ref, bf16[8,5760]{1,0:T(8,128)(2,1)S(1)} %collective-permute-done.17.refs_0_, bf16[8,5760]{1,0:T(8,128)(2,1)S(1)} %collective-permute-done.18.refs_1_, ...), custom_call_target="tpu_custom_call" | custom-call | flops 56623104 | bytes 3538944 | tf_op jit(solution)/shard_map/apply_steps/pallas_call | solution.py:113
  151.4 1.9 apply_steps.7
  153.3 1.6 collective-permute-start.26
  155.7 4.8 %collective-permute-done.22.refs_5_ = bf16[128,1152]{1,0:T(8,128)(2,1)S(1)} collective-permute-done((bf16[128,1152]{1,0:T(8,128)(2,1)S(1)}, bf16[128,1152]{1,0:T(8,128)(2,1)S(1)}, u32[]{:S(2)}, u32[]{:S(2)}) %collective-permute-start.22) | collective-permute-done | bytes 294944 | tf_op jit(solution)/shard_map/ppermute | solution.py:18
  160.5 1.5 collective-permute-start.32
  162.0 4.8 %collective-permute-done.24.refs_7_ = bf16[128,1152]{1,0:T(8,128)(2,1)S(1)} collective-permute-done((bf16[128,1152]{1,0:T(8,128)(2,1)S(1)}, bf16[128,1152]{1,0:T(8,128)(2,1)S(1)}, u32[]{:S(2)}, u32[]{:S(2)}) %collective-permute-start.24) | collective-permute-done | bytes 294944 | tf_op jit(solution)/shard_map/ppermute | solution.py:18
  166.8 1.5 collective-permute-start.34
  168.3 4.8 %collective-permute-done.28 = bf16[128,1152]{1,0:T(8,128)(2,1)S(1)} collective-permute-done((bf16[128,1152]{1,0:T(8,128)(2,1)S(1)}, bf16[128,1152]{1,0:T(8,128)(2,1)S(1)}, u32[]{:S(2)}, u32[]{:S(2)}) %collective-permute-start.28) | collective-permute-done | bytes 294944 | tf_op jit(solution)/shard_map/ppermute | solution.py:18
  173.1 1.5 collective-permute-start.36
  174.7 4.7 %collective-permute-done.26.refs_9_ = bf16[128,1152]{1,0:T(8,128)(2,1)S(1)} collective-permute-done((bf16[128,1152]{1,0:T(8,128)(2,1)S(1)}, bf16[128,1152]{1,0:T(8,128)(2,1)S(1)}, u32[]{:S(2)}, u32[]{:S(2)}) %collective-permute-start.26) | collective-permute-done | bytes 294944 | tf_op jit(solution)/shard_map/ppermute | solution.py:18
  179.4 2.9 %apply_steps.4 = bf16[1152,1152]{1,0:T(8,128)(2,1)} custom-call(s32[1]{0:T(128)} %bitcast.8.at_ref, f32[2]{0:T(128)S(1)} %broadcast_multiply_fusion.1.rate_ref, bf16[8,5760]{1,0:T(8,128)(2,1)S(1)} %collective-permute-done.17.refs_0_, bf16[8,5760]{1,0:T(8,128)(2,1)S(1)} %collective-permute-done.18.refs_1_, ...), custom_call_target="tpu_custom_call" | custom-call | flops 84934656 | bytes 5308416 | tf_op jit(solution)/shard_map/apply_steps/pallas_call | solution.py:113
  182.3 3.4 %collective-permute-done.30.refs_3_ = bf16[128,1152]{1,0:T(8,128)(2,1)S(1)} collective-permute-done((bf16[128,1152]{1,0:T(8,128)(2,1)S(1)}, bf16[128,1152]{1,0:T(8,128)(2,1)S(1)}, u32[]{:S(2)}, u32[]{:S(2)}) %collective-permute-start.30) | collective-permute-done | bytes 294944 | tf_op jit(solution)/shard_map/ppermute | solution.py:18
  185.8 6.3 %collective-permute-done.32.refs_5_ = bf16[128,1152]{1,0:T(8,128)(2,1)S(1)} collective-permute-done((bf16[128,1152]{1,0:T(8,128)(2,1)S(1)}, bf16[128,1152]{1,0:T(8,128)(2,1)S(1)}, u32[]{:S(2)}, u32[]{:S(2)}) %collective-permute-start.32) | collective-permute-done | bytes 294944 | tf_op jit(solution)/shard_map/ppermute | solution.py:18
  192.1 6.3 %collective-permute-done.34.refs_7_ = bf16[128,1152]{1,0:T(8,128)(2,1)S(1)} collective-permute-done((bf16[128,1152]{1,0:T(8,128)(2,1)S(1)}, bf16[128,1152]{1,0:T(8,128)(2,1)S(1)}, u32[]{:S(2)}, u32[]{:S(2)}) %collective-permute-start.34) | collective-permute-done | bytes 294944 | tf_op jit(solution)/shard_map/ppermute | solution.py:18
  198.4 4.3 %collective-permute-done.36.refs_9_ = bf16[128,1152]{1,0:T(8,128)(2,1)S(1)} collective-permute-done((bf16[128,1152]{1,0:T(8,128)(2,1)S(1)}, bf16[128,1152]{1,0:T(8,128)(2,1)S(1)}, u32[]{:S(2)}, u32[]{:S(2)}) %collective-permute-start.36) | collective-permute-done | bytes 294944 | tf_op jit(solution)/shard_map/ppermute | solution.py:18
  202.7 2.9 %apply_steps.5 = bf16[1152,1152]{1,0:T(8,128)(2,1)} custom-call(s32[1]{0:T(128)} %bitcast.8.at_ref, f32[2]{0:T(128)S(1)} %broadcast_multiply_fusion.1.rate_ref, bf16[8,5760]{1,0:T(8,128)(2,1)S(1)} %collective-permute-done.17.refs_0_, bf16[8,5760]{1,0:T(8,128)(2,1)S(1)} %collective-permute-done.18.refs_1_, ...), custom_call_target="tpu_custom_call" | custom-call | flops 84934656 | bytes 5308416 | tf_op jit(solution)/shard_map/apply_steps/pallas_call | solution.py:113
  (120 shorter events, 27.2 us)
Async XLA Ops:
  1.4 26.6 %collective-permute-start = (f32[4,1152]{1,0:T(4,128)S(1)}, f32[4,1152]{1,0:T(4,128)S(1)}, u32[]{:S(2)}, u32[]{:S(2)}) collective-permute-start(f32[4,1152]{1,0:T(4,128)S(1)} %pad_maximum_fusion.1), channel_id=1, source_target_pairs={{0,12},{4,0},{8,4},{12,8},{1,13},{5,1},{9,5},{13,9},{2,14},{6,2},{... | collective-permute-start | bytes 55304 | tf_op jit(solution)/shard_map/ppermute | solution.py:18
  3.8 16.6 %collective-permute-start.4 = (f32[4,1152]{1,0:T(4,128)S(1)}, f32[4,1152]{1,0:T(4,128)S(1)}, u32[]{:S(2)}, u32[]{:S(2)}) collective-permute-start(f32[4,1152]{1,0:T(4,128)S(1)} %pad_maximum_fusion.1), channel_id=1, source_target_pairs={{0,1},{1,2},{2,3},{3,0},{4,5},{5,6},{6,7},{7,4},{8,9},{9,10},{10,1... | collective-permute-start | bytes 55304 | tf_op jit(solution)/shard_map/ppermute | solution.py:18
  5.4 16.5 %collective-permute-start.5 = (f32[4,1152]{1,0:T(4,128)S(1)}, f32[4,1152]{1,0:T(4,128)S(1)}, u32[]{:S(2)}, u32[]{:S(2)}) collective-permute-start(f32[4,1152]{1,0:T(4,128)S(1)} %pad_maximum_fusion.1), channel_id=1, source_target_pairs={{0,2},{1,3},{2,0},{3,1},{4,6},{5,7},{6,4},{7,5},{8,10},{9,11},{10,... | collective-permute-start | bytes 55304 | tf_op jit(solution)/shard_map/ppermute | solution.py:18
  8.0 13.9 %collective-permute-start.6 = (f32[4,1152]{1,0:T(4,128)S(1)}, f32[4,1152]{1,0:T(4,128)S(1)}, u32[]{:S(2)}, u32[]{:S(2)}) collective-permute-start(f32[4,1152]{1,0:T(4,128)S(1)} %pad_maximum_fusion.1), channel_id=1, source_target_pairs={{0,3},{1,0},{2,1},{3,2},{4,7},{5,4},{6,5},{7,6},{8,11},{9,8},{10,9... | collective-permute-start | bytes 55304 | tf_op jit(solution)/shard_map/ppermute | solution.py:18
  9.3 4.0 %copy-start.12 = (s32[2,4]{1,0:T(2,128)S(1)}, s32[2,4]{1,0:T(2,128)}, u32[]{:S(2)}) copy-start(s32[2,4]{1,0:T(2,128)} %param.13) | copy-start | bytes 100
  9.3 4.7 %copy-start.13 = (s32[4]{0:T(128)S(1)}, s32[4]{0:T(128)}, u32[]{:S(2)}) copy-start(s32[4]{0:T(128)} %param.14) | copy-start | bytes 52
  9.3 7.4 %copy-start.14 = (f32[4]{0:T(128)S(1)}, f32[4]{0:T(128)}, u32[]{:S(2)}) copy-start(f32[4]{0:T(128)} %param.15) | copy-start | bytes 52
  9.3 12.6 %copy-start.10 = (f32[1,2,1152]{2,1,0:T(2,128)S(1)}, f32[1,2,1152]{2,1,0:T(2,128)}, u32[]{:S(2)}) copy-start(f32[1,2,1152]{2,1,0:T(2,128)} %param.9) | copy-start | bytes 27652
  9.3 12.6 %copy-start.11 = (f32[1,2,1152]{2,1,0:T(2,128)S(1)}, f32[1,2,1152]{2,1,0:T(2,128)}, u32[]{:S(2)}) copy-start(f32[1,2,1152]{2,1,0:T(2,128)} %param.8) | copy-start | bytes 27652
  12.7 62.4 %collective-permute-start.19 = (bf16[128,1152]{1,0:T(8,128)(2,1)}, bf16[128,1152]{1,0:T(8,128)(2,1)S(1)}, u32[]{:S(2)}, u32[]{:S(2)}) collective-permute-start(bf16[128,1152]{1,0:T(8,128)(2,1)} %get-tuple-element.35), channel_id=1, source_target_pairs={{0,8},{4,12},{8,0},{12,4},{1,9},{5,13},{9,1},{13,5},{2,10},{6,14},... | collective-permute-start | bytes 884744 | tf_op jit(solution)/shard_map/ppermute | solution.py:18
  20.4 55.9 %collective-permute-start.21 = (bf16[128,1152]{1,0:T(8,128)(2,1)}, bf16[128,1152]{1,0:T(8,128)(2,1)S(1)}, u32[]{:S(2)}, u32[]{:S(2)}) collective-permute-start(bf16[128,1152]{1,0:T(8,128)(2,1)} %get-tuple-element.34), channel_id=1, source_target_pairs={{0,8},{4,12},{8,0},{12,4},{1,9},{5,13},{9,1},{13,5},{2,10},{6,14},... | collective-permute-start | bytes 884744 | tf_op jit(solution)/shard_map/ppermute | solution.py:18
  22.1 8.3 %copy-start = (bf16[1,1152,1152]{2,1,0:T(8,128)(2,1)S(1)}, bf16[1,1152,1152]{2,1,0:T(8,128)(2,1)}, u32[]{:S(2)}) copy-start(bf16[1,1152,1152]{2,1,0:T(8,128)(2,1)} %param.12) | copy-start | bytes 7962628
  28.0 3.8 %collective-permute-start.3 = (f32[4,1152]{1,0:T(4,128)S(1)}, f32[4,1152]{1,0:T(4,128)S(1)}, u32[]{:S(2)}, u32[]{:S(2)}) collective-permute-start(f32[4,1152]{1,0:T(4,128)S(1)} %collective-permute-done), channel_id=1, source_target_pairs={{0,3},{1,0},{2,1},{3,2},{4,7},{5,4},{6,5},{7,6},{8,11},{9,8},{10,9... | collective-permute-start | bytes 55304 | tf_op jit(solution)/shard_map/ppermute | solution.py:18
  28.5 4.7 %collective-permute-start.2 = (f32[4,1152]{1,0:T(4,128)S(1)}, f32[4,1152]{1,0:T(4,128)S(1)}, u32[]{:S(2)}, u32[]{:S(2)}) collective-permute-start(f32[4,1152]{1,0:T(4,128)S(1)} %collective-permute-done), channel_id=1, source_target_pairs={{0,2},{1,3},{2,0},{3,1},{4,6},{5,7},{6,4},{7,5},{8,10},{9,11},{10,... | collective-permute-start | bytes 55304 | tf_op jit(solution)/shard_map/ppermute | solution.py:18
  30.2 5.7 %collective-permute-start.1 = (f32[4,1152]{1,0:T(4,128)S(1)}, f32[4,1152]{1,0:T(4,128)}, u32[]{:S(2)}, u32[]{:S(2)}) collective-permute-start(f32[4,1152]{1,0:T(4,128)S(1)} %collective-permute-done), channel_id=1, source_target_pairs={{0,1},{1,2},{2,3},{3,0},{4,5},{5,6},{6,7},{7,4},{8,9},{9,10},{10,1... | collective-permute-start | bytes 55304 | tf_op jit(solution)/shard_map/ppermute | solution.py:18
  31.8 9.7 %collective-permute-start.7 = (f32[8,1152]{1,0:T(8,128)S(1)}, f32[8,1152]{1,0:T(8,128)}, u32[]{:S(2)}, u32[]{:S(2)}) collective-permute-start(f32[8,1152]{1,0:T(8,128)S(1)} %fusion.20), channel_id=1, source_target_pairs={{0,1},{1,2},{2,3},{3,0},{4,5},{5,6},{6,7},{7,4},{8,9},{9,10},{10,1... | collective-permute-start | bytes 110600 | tf_op jit(solution)/shard_map/ppermute | solution.py:18
  33.1 9.1 %collective-permute-start.8 = (f32[8,1152]{1,0:T(8,128)S(1)}, f32[8,1152]{1,0:T(8,128)}, u32[]{:S(2)}, u32[]{:S(2)}) collective-permute-start(f32[8,1152]{1,0:T(8,128)S(1)} %fusion.20), channel_id=1, source_target_pairs={{0,2},{1,3},{2,0},{3,1},{4,6},{5,7},{6,4},{7,5},{8,10},{9,11},{10,... | collective-permute-start | bytes 110600 | tf_op jit(solution)/shard_map/ppermute | solution.py:18
  35.8 4.1 %collective-permute-start.9 = (f32[8,1152]{1,0:T(8,128)S(1)}, f32[8,1152]{1,0:T(8,128)}, u32[]{:S(2)}, u32[]{:S(2)}) collective-permute-start(f32[8,1152]{1,0:T(8,128)S(1)} %fusion.20), channel_id=1, source_target_pairs={{0,3},{1,0},{2,1},{3,2},{4,7},{5,4},{6,5},{7,6},{8,11},{9,8},{10,9... | collective-permute-start | bytes 110600 | tf_op jit(solution)/shard_map/ppermute | solution.py:18
  38.0 7.4 %copy-start.1 = (bf16[1,1152,1152]{2,1,0:T(8,128)(2,1)S(1)}, bf16[1,1152,1152]{2,1,0:T(8,128)(2,1)}, u32[]{:S(2)}) copy-start(bf16[1,1152,1152]{2,1,0:T(8,128)(2,1)} %param.10) | copy-start | bytes 7962628
  45.4 1.8 copy-start.2
  51.2 8.0 %collective-permute-start.12 = (f32[8,1152]{1,0:T(8,128)S(1)}, f32[8,1152]{1,0:T(8,128)S(1)}, u32[]{:S(2)}, u32[]{:S(2)}) collective-permute-start(f32[8,1152]{1,0:T(8,128)S(1)} %convolution_multiply_fusion.4), channel_id=1, source_target_pairs={{0,3},{1,0},{2,1},{3,2},{4,7},{5,4},{6,5},{7,6},{8,11},{9,8},{10,9... | collective-permute-start | bytes 110600 | tf_op jit(solution)/shard_map/ppermute | solution.py:18
  54.3 4.9 %collective-permute-start.11 = (f32[8,1152]{1,0:T(8,128)S(1)}, f32[8,1152]{1,0:T(8,128)S(1)}, u32[]{:S(2)}, u32[]{:S(2)}) collective-permute-start(f32[8,1152]{1,0:T(8,128)S(1)} %convolution_multiply_fusion.4), channel_id=1, source_target_pairs={{0,2},{1,3},{2,0},{3,1},{4,6},{5,7},{6,4},{7,5},{8,10},{9,11},{10,... | collective-permute-start | bytes 110600 | tf_op jit(solution)/shard_map/ppermute | solution.py:18
  54.3 5.8 %collective-permute-start.10 = (f32[8,1152]{1,0:T(8,128)S(1)}, f32[8,1152]{1,0:T(8,128)S(1)}, u32[]{:S(2)}, u32[]{:S(2)}) collective-permute-start(f32[8,1152]{1,0:T(8,128)S(1)} %convolution_multiply_fusion.4), channel_id=1, source_target_pairs={{0,1},{1,2},{2,3},{3,0},{4,5},{5,6},{6,7},{7,4},{8,9},{9,10},{10,1... | collective-permute-start | bytes 110600 | tf_op jit(solution)/shard_map/ppermute | solution.py:18
  60.9 11.4 %copy-start.9 = (bf16[128,1152]{1,0:T(8,128)(2,1)S(1)}, bf16[128,1152]{1,0:T(8,128)(2,1)}, u32[]{:S(2)}) copy-start(bf16[128,1152]{1,0:T(8,128)(2,1)} %get-tuple-element.33) | copy-start | bytes 884740
  60.9 12.1 %copy-start.8 = (bf16[128,1152]{1,0:T(8,128)(2,1)S(1)}, bf16[128,1152]{1,0:T(8,128)(2,1)}, u32[]{:S(2)}) copy-start(bf16[128,1152]{1,0:T(8,128)(2,1)} %get-tuple-element.36) | copy-start | bytes 884740
  60.9 13.4 %copy-start.7 = (bf16[128,1152]{1,0:T(8,128)(2,1)S(1)}, bf16[128,1152]{1,0:T(8,128)(2,1)}, u32[]{:S(2)}) copy-start(bf16[128,1152]{1,0:T(8,128)(2,1)} %get-tuple-element.32) | copy-start | bytes 884740
  60.9 14.1 %copy-start.6 = (bf16[128,1152]{1,0:T(8,128)(2,1)S(1)}, bf16[128,1152]{1,0:T(8,128)(2,1)}, u32[]{:S(2)}) copy-start(bf16[128,1152]{1,0:T(8,128)(2,1)} %get-tuple-element.31) | copy-start | bytes 884740
  60.9 15.4 %copy-start.5 = (bf16[128,1152]{1,0:T(8,128)(2,1)S(1)}, bf16[128,1152]{1,0:T(8,128)(2,1)}, u32[]{:S(2)}) copy-start(bf16[128,1152]{1,0:T(8,128)(2,1)} %get-tuple-element.30) | copy-start | bytes 884740
  61.4 20.7 %copy-start.4 = (bf16[128,1152]{1,0:T(8,128)(2,1)S(1)}, bf16[128,1152]{1,0:T(8,128)(2,1)}, u32[]{:S(2)}) copy-start(bf16[128,1152]{1,0:T(8,128)(2,1)} %get-tuple-element.37) | copy-start | bytes 884740
  61.5 81.8 %copy-start.3 = (bf16[128,1152]{1,0:T(8,128)(2,1)S(1)}, bf16[128,1152]{1,0:T(8,128)(2,1)}, u32[]{:S(2)}) copy-start(bf16[128,1152]{1,0:T(8,128)(2,1)} %get-tuple-element.29) | copy-start | bytes 884740
  62.0 3.7 %collective-permute-start.15 = (f32[2,1152]{1,0:T(2,128)S(1)}, f32[2,1152]{1,0:T(2,128)S(1)}, u32[]{:S(2)}, u32[]{:S(2)}) collective-permute-start(f32[2,1152]{1,0:T(2,128)S(1)} %get-tuple-element.41), channel_id=1, source_target_pairs={{0,3},{1,0},{2,1},{3,2},{4,7},{5,4},{6,5},{7,6},{8,11},{9,8},{10,9... | collective-permute-start | bytes 27656 | tf_op jit(solution)/shard_map/ppermute | solution.py:18
  62.6 4.6 %collective-permute-start.14 = (f32[2,1152]{1,0:T(2,128)S(1)}, f32[2,1152]{1,0:T(2,128)S(1)}, u32[]{:S(2)}, u32[]{:S(2)}) collective-permute-start(f32[2,1152]{1,0:T(2,128)S(1)} %get-tuple-element.42), channel_id=1, source_target_pairs={{0,2},{1,3},{2,0},{3,1},{4,6},{5,7},{6,4},{7,5},{8,10},{9,11},{10,... | collective-permute-start | bytes 27656 | tf_op jit(solution)/shard_map/ppermute | solution.py:18
  63.4 5.5 %collective-permute-start.13 = (f32[2,1152]{1,0:T(2,128)S(1)}, f32[2,1152]{1,0:T(2,128)S(1)}, u32[]{:S(2)}, u32[]{:S(2)}) collective-permute-start(f32[2,1152]{1,0:T(2,128)S(1)} %get-tuple-element.40), channel_id=1, source_target_pairs={{0,1},{1,2},{2,3},{3,0},{4,5},{5,6},{6,7},{7,4},{8,9},{9,10},{10,1... | collective-permute-start | bytes 27656 | tf_op jit(solution)/shard_map/ppermute | solution.py:18
  65.7 7.3 %collective-permute-start.17 = (bf16[8,5760]{1,0:T(8,128)(2,1)S(1)}, bf16[8,5760]{1,0:T(8,128)(2,1)S(1)}, u32[]{:S(2)}, u32[]{:S(2)}) collective-permute-start(bf16[8,5760]{1,0:T(8,128)(2,1)S(1)} %constant_dynamic-update-slice_fusion), channel_id=1, source_target_pairs={{0,8},{4,12},{8,0},{12,4},{1,9},{5,13},{9,1},{13,5},{2,10},{6,14},... | collective-permute-start | bytes 276488 | tf_op jit(solution)/shard_map/ppermute | solution.py:18
  67.1 7.2 %collective-permute-start.18 = (bf16[8,5760]{1,0:T(8,128)(2,1)S(1)}, bf16[8,5760]{1,0:T(8,128)(2,1)S(1)}, u32[]{:S(2)}, u32[]{:S(2)}) collective-permute-start(bf16[8,5760]{1,0:T(8,128)(2,1)S(1)} %constant_dynamic-update-slice_fusion.5), channel_id=1, source_target_pairs={{0,8},{4,12},{8,0},{12,4},{1,9},{5,13},{9,1},{13,5},{2,10},{6,14},... | collective-permute-start | bytes 276488 | tf_op jit(solution)/shard_map/ppermute | solution.py:18
  68.9 3.4 %collective-permute-start.16 = (f32[4,1152]{1,0:T(4,128)S(1)}, f32[4,1152]{1,0:T(4,128)S(1)}, u32[]{:S(2)}, u32[]{:S(2)}) collective-permute-start(f32[4,1152]{1,0:T(4,128)S(1)} %pad_maximum_fusion.2), channel_id=1, source_target_pairs={{0,4},{4,8},{8,12},{12,0},{1,5},{5,9},{9,13},{13,1},{2,6},{6,10},{... | collective-permute-start | bytes 55304 | tf_op jit(solution)/shard_map/ppermute | solution.py:18
  72.3 9.9 %collective-permute-start.23 = (bf16[128,1152]{1,0:T(8,128)(2,1)S(1)}, bf16[128,1152]{1,0:T(8,128)(2,1)S(1)}, u32[]{:S(2)}, u32[]{:S(2)}) collective-permute-start(bf16[128,1152]{1,0:T(8,128)(2,1)S(1)} %copy-done.9), channel_id=1, source_target_pairs={{0,8},{4,12},{8,0},{12,4},{1,9},{5,13},{9,1},{13,5},{2,10},{6,14},... | collective-permute-start | bytes 884744 | tf_op jit(solution)/shard_map/ppermute | solution.py:18
  73.0 15.5 %collective-permute-start.25 = (bf16[128,1152]{1,0:T(8,128)(2,1)S(1)}, bf16[128,1152]{1,0:T(8,128)(2,1)S(1)}, u32[]{:S(2)}, u32[]{:S(2)}) collective-permute-start(bf16[128,1152]{1,0:T(8,128)(2,1)S(1)} %copy-done.8), channel_id=1, source_target_pairs={{0,8},{4,12},{8,0},{12,4},{1,9},{5,13},{9,1},{13,5},{2,10},{6,14},... | collective-permute-start | bytes 884744 | tf_op jit(solution)/shard_map/ppermute | solution.py:18
  74.3 20.5 %collective-permute-start.27 = (bf16[128,1152]{1,0:T(8,128)(2,1)S(1)}, bf16[128,1152]{1,0:T(8,128)(2,1)S(1)}, u32[]{:S(2)}, u32[]{:S(2)}) collective-permute-start(bf16[128,1152]{1,0:T(8,128)(2,1)S(1)} %copy-done.7), channel_id=1, source_target_pairs={{0,8},{4,12},{8,0},{12,4},{1,9},{5,13},{9,1},{13,5},{2,10},{6,14},... | collective-permute-start | bytes 884744 | tf_op jit(solution)/shard_map/ppermute | solution.py:18
  75.1 26.1 %collective-permute-start.29 = (bf16[128,1152]{1,0:T(8,128)(2,1)S(1)}, bf16[128,1152]{1,0:T(8,128)(2,1)S(1)}, u32[]{:S(2)}, u32[]{:S(2)}) collective-permute-start(bf16[128,1152]{1,0:T(8,128)(2,1)S(1)} %copy-done.6), channel_id=1, source_target_pairs={{0,8},{4,12},{8,0},{12,4},{1,9},{5,13},{9,1},{13,5},{2,10},{6,14},... | collective-permute-start | bytes 884744 | tf_op jit(solution)/shard_map/ppermute | solution.py:18
  76.4 31.1 %collective-permute-start.31 = (bf16[128,1152]{1,0:T(8,128)(2,1)S(1)}, bf16[128,1152]{1,0:T(8,128)(2,1)S(1)}, u32[]{:S(2)}, u32[]{:S(2)}) collective-permute-start(bf16[128,1152]{1,0:T(8,128)(2,1)S(1)} %copy-done.5), channel_id=1, source_target_pairs={{0,8},{4,12},{8,0},{12,4},{1,9},{5,13},{9,1},{13,5},{2,10},{6,14},... | collective-permute-start | bytes 884744 | tf_op jit(solution)/shard_map/ppermute | solution.py:18
  82.2 31.6 %collective-permute-start.33 = (bf16[128,1152]{1,0:T(8,128)(2,1)S(1)}, bf16[128,1152]{1,0:T(8,128)(2,1)S(1)}, u32[]{:S(2)}, u32[]{:S(2)}) collective-permute-start(bf16[128,1152]{1,0:T(8,128)(2,1)S(1)} %copy-done.4), channel_id=1, source_target_pairs={{0,8},{4,12},{8,0},{12,4},{1,9},{5,13},{9,1},{13,5},{2,10},{6,14},... | collective-permute-start | bytes 884744 | tf_op jit(solution)/shard_map/ppermute | solution.py:18
  88.5 31.6 %collective-permute-start.37 = (bf16[128,1152]{1,0:T(8,128)(2,1)S(1)}, bf16[128,1152]{1,0:T(8,128)(2,1)S(1)}, u32[]{:S(2)}, u32[]{:S(2)}) collective-permute-start(bf16[128,1152]{1,0:T(8,128)(2,1)S(1)} %get-tuple-element.27), channel_id=1, source_target_pairs={{0,8},{4,12},{8,0},{12,4},{1,9},{5,13},{9,1},{13,5},{2,10},{6,14},... | collective-permute-start | bytes 884744 | tf_op jit(solution)/shard_map/ppermute | solution.py:18
  94.8 31.6 %collective-permute-start.40 = (bf16[128,1152]{1,0:T(8,128)(2,1)S(1)}, bf16[128,1152]{1,0:T(8,128)(2,1)S(1)}, u32[]{:S(2)}, u32[]{:S(2)}) collective-permute-start(bf16[128,1152]{1,0:T(8,128)(2,1)S(1)} %get-tuple-element.25), channel_id=1, source_target_pairs={{0,8},{4,12},{8,0},{12,4},{1,9},{5,13},{9,1},{13,5},{2,10},{6,14},... | collective-permute-start | bytes 884744 | tf_op jit(solution)/shard_map/ppermute | solution.py:18
  101.2 31.6 %collective-permute-start.42 = (bf16[128,1152]{1,0:T(8,128)(2,1)S(1)}, bf16[128,1152]{1,0:T(8,128)(2,1)S(1)}, u32[]{:S(2)}, u32[]{:S(2)}) collective-permute-start(bf16[128,1152]{1,0:T(8,128)(2,1)S(1)} %get-tuple-element.28), channel_id=1, source_target_pairs={{0,8},{4,12},{8,0},{12,4},{1,9},{5,13},{9,1},{13,5},{2,10},{6,14},... | collective-permute-start | bytes 884744 | tf_op jit(solution)/shard_map/ppermute | solution.py:18
  107.5 31.6 %collective-permute-start.44 = (bf16[128,1152]{1,0:T(8,128)(2,1)S(1)}, bf16[128,1152]{1,0:T(8,128)(2,1)S(1)}, u32[]{:S(2)}, u32[]{:S(2)}) collective-permute-start(bf16[128,1152]{1,0:T(8,128)(2,1)S(1)} %get-tuple-element.24), channel_id=1, source_target_pairs={{0,8},{4,12},{8,0},{12,4},{1,9},{5,13},{9,1},{13,5},{2,10},{6,14},... | collective-permute-start | bytes 884744 | tf_op jit(solution)/shard_map/ppermute | solution.py:18
  113.8 29.5 %collective-permute-start.39 = (bf16[128,1152]{1,0:T(8,128)(2,1)S(1)}, bf16[128,1152]{1,0:T(8,128)(2,1)S(1)}, u32[]{:S(2)}, u32[]{:S(2)}) collective-permute-start(bf16[128,1152]{1,0:T(8,128)(2,1)S(1)} %get-tuple-element.26), channel_id=1, source_target_pairs={{0,8},{4,12},{8,0},{12,4},{1,9},{5,13},{9,1},{13,5},{2,10},{6,14},... | collective-permute-start | bytes 884744 | tf_op jit(solution)/shard_map/ppermute | solution.py:18
  120.1 24.2 %collective-permute-start.38 = (bf16[128,1152]{1,0:T(8,128)(2,1)S(1)}, bf16[128,1152]{1,0:T(8,128)(2,1)S(1)}, u32[]{:S(2)}, u32[]{:S(2)}) collective-permute-start(bf16[128,1152]{1,0:T(8,128)(2,1)S(1)} %collective-permute-done.37.refs_2_), channel_id=1, source_target_pairs={{0,16},{16,0},{1,17},{17,1},{2,18},{18,2},{3,19},{19,3},{4,20},{20... | collective-permute-start | bytes 884744 | tf_op jit(solution)/shard_map/ppermute | solution.py:18
  126.4 19.4 %collective-permute-start.41 = (bf16[128,1152]{1,0:T(8,128)(2,1)S(1)}, bf16[128,1152]{1,0:T(8,128)(2,1)S(1)}, u32[]{:S(2)}, u32[]{:S(2)}) collective-permute-start(bf16[128,1152]{1,0:T(8,128)(2,1)S(1)} %collective-permute-done.40.refs_2_), channel_id=1, source_target_pairs={{0,16},{16,0},{1,17},{17,1},{2,18},{18,2},{3,19},{19,3},{4,20},{20... | collective-permute-start | bytes 884744 | tf_op jit(solution)/shard_map/ppermute | solution.py:18
  132.7 13.6 %collective-permute-start.43 = (bf16[128,1152]{1,0:T(8,128)(2,1)S(1)}, bf16[128,1152]{1,0:T(8,128)(2,1)S(1)}, u32[]{:S(2)}, u32[]{:S(2)}) collective-permute-start(bf16[128,1152]{1,0:T(8,128)(2,1)S(1)} %collective-permute-done.42.refs_4_), channel_id=1, source_target_pairs={{0,16},{16,0},{1,17},{17,1},{2,18},{18,2},{3,19},{19,3},{4,20},{20... | collective-permute-start | bytes 884744 | tf_op jit(solution)/shard_map/ppermute | solution.py:18
  139.1 8.8 %collective-permute-start.45 = (bf16[128,1152]{1,0:T(8,128)(2,1)S(1)}, bf16[128,1152]{1,0:T(8,128)(2,1)S(1)}, u32[]{:S(2)}, u32[]{:S(2)}) collective-permute-start(bf16[128,1152]{1,0:T(8,128)(2,1)S(1)} %collective-permute-done.44.refs_6_), channel_id=1, source_target_pairs={{0,16},{16,0},{1,17},{17,1},{2,18},{18,2},{3,19},{19,3},{4,20},{20... | collective-permute-start | bytes 884744 | tf_op jit(solution)/shard_map/ppermute | solution.py:18
  143.3 10.1 %collective-permute-start.35 = (bf16[128,1152]{1,0:T(8,128)(2,1)S(1)}, bf16[128,1152]{1,0:T(8,128)(2,1)S(1)}, u32[]{:S(2)}, u32[]{:S(2)}) collective-permute-start(bf16[128,1152]{1,0:T(8,128)(2,1)S(1)} %copy-done.3), channel_id=1, source_target_pairs={{0,8},{4,12},{8,0},{12,4},{1,9},{5,13},{9,1},{13,5},{2,10},{6,14},... | collective-permute-start | bytes 884744 | tf_op jit(solution)/shard_map/ppermute | solution.py:18
  144.3 10.6 %collective-permute-start.20 = (bf16[128,1152]{1,0:T(8,128)(2,1)S(1)}, bf16[128,1152]{1,0:T(8,128)(2,1)S(1)}, u32[]{:S(2)}, u32[]{:S(2)}) collective-permute-start(bf16[128,1152]{1,0:T(8,128)(2,1)S(1)} %collective-permute-done.19.refs_2_), channel_id=1, source_target_pairs={{0,16},{16,0},{1,17},{17,1},{2,18},{18,2},{3,19},{19,3},{4,20},{20... | collective-permute-start | bytes 884744 | tf_op jit(solution)/shard_map/ppermute | solution.py:18
  145.8 14.7 %collective-permute-start.22 = (bf16[128,1152]{1,0:T(8,128)(2,1)S(1)}, bf16[128,1152]{1,0:T(8,128)(2,1)S(1)}, u32[]{:S(2)}, u32[]{:S(2)}) collective-permute-start(bf16[128,1152]{1,0:T(8,128)(2,1)S(1)} %collective-permute-done.21.refs_4_), channel_id=1, source_target_pairs={{0,16},{16,0},{1,17},{17,1},{2,18},{18,2},{3,19},{19,3},{4,20},{20... | collective-permute-start | bytes 884744 | tf_op jit(solution)/shard_map/ppermute | solution.py:18
  146.3 20.5 %collective-permute-start.24 = (bf16[128,1152]{1,0:T(8,128)(2,1)S(1)}, bf16[128,1152]{1,0:T(8,128)(2,1)S(1)}, u32[]{:S(2)}, u32[]{:S(2)}) collective-permute-start(bf16[128,1152]{1,0:T(8,128)(2,1)S(1)} %collective-permute-done.23.refs_6_), channel_id=1, source_target_pairs={{0,16},{16,0},{1,17},{17,1},{2,18},{18,2},{3,19},{19,3},{4,20},{20... | collective-permute-start | bytes 884744 | tf_op jit(solution)/shard_map/ppermute | solution.py:18
  147.8 25.3 %collective-permute-start.28 = (bf16[128,1152]{1,0:T(8,128)(2,1)S(1)}, bf16[128,1152]{1,0:T(8,128)(2,1)S(1)}, u32[]{:S(2)}, u32[]{:S(2)}) collective-permute-start(bf16[128,1152]{1,0:T(8,128)(2,1)S(1)} %collective-permute-done.27), channel_id=1, source_target_pairs={{0,16},{16,0},{1,17},{17,1},{2,18},{18,2},{3,19},{19,3},{4,20},{20... | collective-permute-start | bytes 884744 | tf_op jit(solution)/shard_map/ppermute | solution.py:18
  153.3 26.1 %collective-permute-start.26 = (bf16[128,1152]{1,0:T(8,128)(2,1)S(1)}, bf16[128,1152]{1,0:T(8,128)(2,1)S(1)}, u32[]{:S(2)}, u32[]{:S(2)}) collective-permute-start(bf16[128,1152]{1,0:T(8,128)(2,1)S(1)} %collective-permute-done.25.refs_8_), channel_id=1, source_target_pairs={{0,16},{16,0},{1,17},{17,1},{2,18},{18,2},{3,19},{19,3},{4,20},{20... | collective-permute-start | bytes 884744 | tf_op jit(solution)/shard_map/ppermute | solution.py:18
  154.9 30.8 %collective-permute-start.30 = (bf16[128,1152]{1,0:T(8,128)(2,1)S(1)}, bf16[128,1152]{1,0:T(8,128)(2,1)S(1)}, u32[]{:S(2)}, u32[]{:S(2)}) collective-permute-start(bf16[128,1152]{1,0:T(8,128)(2,1)S(1)} %collective-permute-done.29.refs_2_), channel_id=1, source_target_pairs={{0,16},{16,0},{1,17},{17,1},{2,18},{18,2},{3,19},{19,3},{4,20},{20... | collective-permute-start | bytes 884744 | tf_op jit(solution)/shard_map/ppermute | solution.py:18
  160.5 31.6 %collective-permute-start.32 = (bf16[128,1152]{1,0:T(8,128)(2,1)S(1)}, bf16[128,1152]{1,0:T(8,128)(2,1)S(1)}, u32[]{:S(2)}, u32[]{:S(2)}) collective-permute-start(bf16[128,1152]{1,0:T(8,128)(2,1)S(1)} %collective-permute-done.31.refs_4_), channel_id=1, source_target_pairs={{0,16},{16,0},{1,17},{17,1},{2,18},{18,2},{3,19},{19,3},{4,20},{20... | collective-permute-start | bytes 884744 | tf_op jit(solution)/shard_map/ppermute | solution.py:18
  166.8 31.6 %collective-permute-start.34 = (bf16[128,1152]{1,0:T(8,128)(2,1)S(1)}, bf16[128,1152]{1,0:T(8,128)(2,1)S(1)}, u32[]{:S(2)}, u32[]{:S(2)}) collective-permute-start(bf16[128,1152]{1,0:T(8,128)(2,1)S(1)} %collective-permute-done.33.refs_6_), channel_id=1, source_target_pairs={{0,16},{16,0},{1,17},{17,1},{2,18},{18,2},{3,19},{19,3},{4,20},{20... | collective-permute-start | bytes 884744 | tf_op jit(solution)/shard_map/ppermute | solution.py:18
  173.1 29.6 %collective-permute-start.36 = (bf16[128,1152]{1,0:T(8,128)(2,1)S(1)}, bf16[128,1152]{1,0:T(8,128)(2,1)S(1)}, u32[]{:S(2)}, u32[]{:S(2)}) collective-permute-start(bf16[128,1152]{1,0:T(8,128)(2,1)S(1)} %collective-permute-done.35.refs_8_), channel_id=1, source_target_pairs={{0,16},{16,0},{1,17},{17,1},{2,18},{18,2},{3,19},{19,3},{4,20},{20... | collective-permute-start | bytes 884744 | tf_op jit(solution)/shard_map/ppermute | solution.py:18
